TPU v7x, 32 devices: a whole 2x2x4 slice. The times are simulated.
32 devices in a mesh: row: 8 (over z, x), col: 4 (over y, core).
Axes of the slice: x: 2, y: 2, z: 4, core: 2. Of those that a mesh axis runs over, the one named last changes fastest.
Arguments:
- mel: float32 [128, 18432], P('col', 'row'), may hold values from -6 to 6
- pair_val: int32 [128], replicated, may hold values from 0 to 31
- pair_cond: int32 [128], replicated, may hold values from 0 to 31
- val_energy: float32 [32], replicated, may hold values from -8 to -1
- cond_energy: float32 [32], replicated, may hold values from 1 to 8
- freqs: float32 [2], replicated, may hold values from 0.5 to 6
Outputs:
- chi: float32 [2, 18432, 18432], P(None, 'row', 'col')
All inputs are finite; a program needn't handle non-finite values.
Results may differ from a plain program's by a relative error of at most 0.000098.
Values sent between devices are 32-bit elements; how exact they have to be, the bound alone decides.
A program may use at most 128 MiB of HBM per device.

v0:
```python
import math

import jax
import jax.numpy as jnp
from jax import lax
from jax.sharding import PartitionSpec as P

PAIRS = 128


def body(mel, pair_val, pair_cond, val_energy, cond_energy, freqs):
    rows_all = lax.all_gather(mel, "col", axis=0, tiled=True)
    own_block = lax.all_gather(mel, "row", axis=1, tiled=True)
    col_block = lax.all_to_all(own_block, "col", split_axis=1, concat_axis=0, tiled=True)
    cond_onehot = (
        pair_cond[:, None] == jnp.arange(cond_energy.shape[0], dtype=jnp.int32)[None, :]
    ).astype(jnp.float32)
    val_onehot = (
        pair_val[:, None] == jnp.arange(val_energy.shape[0], dtype=jnp.int32)[None, :]
    ).astype(jnp.float32)
    gap = jnp.sum(cond_onehot * cond_energy[None, :], axis=1) - jnp.sum(
        val_onehot * val_energy[None, :], axis=1
    )
    scale = 1.0 / math.sqrt(PAIRS)
    weights = (
        -4.0
        * gap[None, :]
        / (gap[None, :] * gap[None, :] + freqs[:, None] * freqs[:, None])
        * scale
    )
    scaled = weights[:, :, None] * rows_all[None, :, :]
    return lax.dot_general(
        scaled,
        col_block,
        (((1,), (0,)), ((), ())),
        precision=lax.Precision.HIGHEST,
        preferred_element_type=jnp.float32,
    )


def solution(mesh):
    return jax.shard_map(
        body,
        mesh=mesh,
        in_specs=(P("col", "row"), P(), P(), P(), P(), P()),
        out_specs=P(None, "row", "col"),
        check_vma=False,
    )
```

profile of v0, /device:TPU:1, one launch (start us, length us, event | category | flops | bytes accessed | tf_op | source)
XLA Modules:
  0.0 184.1 jit_solution(5742177264491357623)
XLA Ops:
  6.5 0.0 all-gather.5.cloned.1.call-start
  6.5 0.7 all-gather.5.cloned.1.call-update
  7.3 0.0 all-gather.3.cloned.1.call-start
  7.3 0.7 all-gather.3.cloned.1.call-update
  8.0 53.9 %all-gather.5.cloned.1.call-done = f32[32,18432]{1,0:T(8,128)} async-done(((f32[32,2304]{1,0:T(8,128)}), f32[32,18432]{1,0:T(8,128)}) %all-gather.5.cloned.1.call-update) | async-done | bytes 2359312 | tf_op jit(solution)/shard_map/all_gather | solution.py:13
  61.9 3.2 %copy.13 = f32[4,4,8,4608]{3,2,0,1:T(8,128)} copy(f32[4,4,8,4608]{3,2,1,0:T(8,128)} %bitcast.13) | data formatting | bytes 4718592 | tf_op jit(solution)/shard_map/all_to_all | solution.py:14
  65.2 0.0 copy-start.4
  65.2 0.0 copy-start
  65.2 0.0 copy-start.1
  65.2 0.0 copy-start.2
  65.2 0.0 copy-start.3
  65.2 5.9 %all-to-all-start = ((f32[32,4,4608]{2,0,1:T(8,128)}), f32[32,4,4608]{2,0,1:T(8,128)S(1)}, u32[]{:S(2)}, u32[]{:S(2)}) async-start(f32[32,4,4608]{2,0,1:T(8,128)} %bitcast.12), calls=%async_computation | async-start | bytes 4718592 | tf_op jit(solution)/shard_map/all_to_all | solution.py:14
  71.1 0.0 copy-done.4
  71.1 0.0 copy-done
  71.2 0.0 copy-done.1
  71.2 0.0 copy-done.2
  71.2 0.0 copy-done.3
  71.2 0.1 select_reduce_fusion
  71.3 0.1 divide_multiply_fusion
  71.4 16.2 %all-gather.3.cloned.1.call-done = f32[128,2304]{1,0:T(8,128)} async-done(((f32[32,2304]{1,0:T(8,128)}), f32[128,2304]{1,0:T(8,128)}) %all-gather.3.cloned.1.call-update) | async-done | bytes 1179664 | tf_op jit(solution)/shard_map/all_gather | solution.py:12
  87.5 1.6 copy.9
  89.2 15.7 %all-to-all-done = f32[32,4,4608]{2,0,1:T(8,128)S(1)} async-done(((f32[32,4,4608]{2,0,1:T(8,128)}), f32[32,4,4608]{2,0,1:T(8,128)S(1)}, u32[]{:S(2)}, u32[]{:S(2)}) %all-to-all-start) | async-done | bytes 2359328 | tf_op jit(solution)/shard_map/all_to_all | solution.py:14
  104.9 72.3 %fusion = f32[2,2304,4608]{2,1,0:T(8,128)} fusion(f32[128,4608,1]{1,0,2:T(8,128)S(1)} %bitcast.11, f32[128,2304]{0,1:T(8,128)S(1)} %copy.9, f32[2,128]{1,0:T(2,128)S(1)} %divide_multiply_fusion), kind=kOutput, calls=%fused_computation.1 | convolution fusion | flops 32615497728 | bytes 88474624 | tf_op jit(solution)/shard_map/dot_general | solution.py:32
  (2 shorter events, 0.0 us)
Async XLA Ops:
  6.5 55.4 %all-gather.5.cloned.1.call-start = ((), (), s32[]{:S(2)}) async-start(), calls=%async_computation.2 | async-start | bytes 2654208 | tf_op jit(solution)/shard_map/all_gather | solution.py:13
  7.3 80.3 %all-gather.3.cloned.1.call-start = ((), (), s32[]{:S(2)}) async-start(), calls=%async_computation.1 | async-start | bytes 1474560 | tf_op jit(solution)/shard_map/all_gather | solution.py:12
  65.2 6.0 %copy-start.4 = (f32[2]{0:T(128)S(1)}, f32[2]{0:T(128)}, u32[]{:S(2)}) copy-start(f32[2]{0:T(128)} %param.11) | copy-start | bytes 28
  65.2 6.0 %copy-start = (f32[32]{0:T(128)S(1)}, f32[32]{0:T(128)}, u32[]{:S(2)}) copy-start(f32[32]{0:T(128)} %param.9) | copy-start | bytes 388
  65.2 6.0 %copy-start.1 = (s32[128]{0:T(128)S(1)}, s32[128]{0:T(128)}, u32[]{:S(2)}) copy-start(s32[128]{0:T(128)} %param.7) | copy-start | bytes 1540
  65.2 6.0 %copy-start.2 = (f32[32]{0:T(128)S(1)}, f32[32]{0:T(128)}, u32[]{:S(2)}) copy-start(f32[32]{0:T(128)} %param.10) | copy-start | bytes 388
  65.2 6.0 %copy-start.3 = (s32[128]{0:T(128)S(1)}, s32[128]{0:T(128)}, u32[]{:S(2)}) copy-start(s32[128]{0:T(128)} %param.8) | copy-start | bytes 1540
  65.2 39.7 %all-to-all-start = ((f32[32,4,4608]{2,0,1:T(8,128)}), f32[32,4,4608]{2,0,1:T(8,128)S(1)}, u32[]{:S(2)}, u32[]{:S(2)}) async-start(f32[32,4,4608]{2,0,1:T(8,128)} %bitcast.12), calls=%async_computation | async-start | bytes 4718592 | tf_op jit(solution)/shard_map/all_to_all | solution.py:14
Sparse Core Ops, SparseCore 0:
  9.5 52.3 all-gather.4
  63.5 23.9 all-gather.2
where the time goes:
time: 185 us; the launch traced here: 184 us
  waiting for transfers between devices  87.2 us (47%)
  matrix products  72.3 us (39%)
  between operations  13.5 us (7%)
  starting transfers between devices  5.98 us (3%)
  local copies, waits for them, and re-layouts  4.89 us (3%)
    dot_general x1, matrix products, body(): lax.dot_general(scaled, col_block, (((1,), (0,)), ((), ())), precision=la...  72.3 us
    all_gather x1, waiting for transfers between devices, body(): own_block = lax.all_gather(mel, 'row', axis=1, tiled=True)  53.9 us
    all_gather x1, waiting for transfers between devices, body(): rows_all = lax.all_gather(mel, 'col', axis=0, tiled=True)  16.2 us
    all_to_all x1, waiting for transfers between devices, body(): lax.all_to_all(own_block, 'col', split_axis=1, concat_axis=0, tiled=True)  15.7 us
    all_to_all x1, starting transfers between devices, body(): lax.all_to_all(own_block, 'col', split_axis=1, concat_axis=0, tiled=True)  5.94 us
  transfers between devices with their start and end apart: 3, of which 3 were waited for; matrix products, arithmetic and copies ran while one was open for 3% of the time, Pallas kernels for 0%

commit v1 on v0

v1 whole, which is shorter than its diff:
```python
import functools
import math

import jax
import jax.numpy as jnp
from jax import lax
from jax.experimental import pallas as pl
from jax.experimental.pallas import tpu as pltpu
from jax.sharding import PartitionSpec as P

PAIRS = 128
MESH = pl.DeviceIdType.MESH
PIECES = 3


def pair_weights(pair_val, pair_cond, val_energy, cond_energy, freqs):
    cond_onehot = (
        pair_cond[:, None] == jnp.arange(cond_energy.shape[0], dtype=jnp.int32)[None, :]
    ).astype(jnp.float32)
    val_onehot = (
        pair_val[:, None] == jnp.arange(val_energy.shape[0], dtype=jnp.int32)[None, :]
    ).astype(jnp.float32)
    gap = jnp.sum(cond_onehot * cond_energy[None, :], axis=1) - jnp.sum(
        val_onehot * val_energy[None, :], axis=1
    )
    scale = 1.0 / math.sqrt(PAIRS)
    return (
        -4.0
        * gap[:, None]
        / (gap[:, None] * gap[:, None] + freqs[None, :] * freqs[None, :])
        * scale
    )


def split(x):
    hi = x.astype(jnp.bfloat16)
    return hi, (x - hi.astype(jnp.float32)).astype(jnp.bfloat16)


def gather_kernel(
    span, w_ref, mel_ref, lhs_ref, rhs_ref, rows, own, other,
    load_sem, row_send, row_recv, up_send, down_send, own_recv, swap_send, swap_recv,
):
    r, c = lax.axis_index("row"), lax.axis_index("col")
    group, place = r // span, r % span
    depth, width = mel_ref.shape
    groups = 4
    pairs = groups * depth
    core = c + 1 - 2 * (c % 2)
    chip = c + 2 - 4 * (c // 2)
    both = core + 2 - 4 * (core // 2)
    beside = r + 1 - 2 * place
    up, down = r + span, r - span
    has_up, has_down = group < groups - 1, group > 0
    source = group == c
    send_up = (group >= c) & has_up
    send_down = (group <= c) & has_down

    load = pltpu.make_async_copy(mel_ref, rows.at[0], load_sem)
    load.start()
    barrier = pltpu.get_barrier_semaphore()
    for device in ((r, core), (r, chip), (beside, c)):
        pl.semaphore_signal(barrier, inc=1, device_id=device, device_id_type=MESH)

    @pl.when(has_up)
    def _():
        pl.semaphore_signal(barrier, inc=1, device_id=(up, c), device_id_type=MESH)

    @pl.when(has_down)
    def _():
        pl.semaphore_signal(barrier, inc=1, device_id=(down, c), device_id_type=MESH)

    pl.semaphore_wait(barrier, 3 + has_up.astype(jnp.int32) + has_down.astype(jnp.int32))
    load.wait()

    step = width // PIECES

    def view(ref, t, p):
        return ref.at[t, :, pl.ds(p * step, step)]

    def send(src, s, dst, t, p, send_sem, recv_sem, device):
        return pltpu.make_async_remote_copy(
            src_ref=view(src, s, p), dst_ref=view(dst, t, p), send_sem=send_sem, recv_sem=recv_sem,
            device_id=device, device_id_type=MESH,
        )

    def row_copy(t, p):
        device = (r, chip) if t == 2 else (r, core)
        return send(rows, 2 if t == 3 else 0, rows, t, p, row_send.at[t - 1, p], row_recv.at[t - 1, p], device)

    def up_copy(src, t, p):
        return send(src, t, own, t, p, up_send.at[t, p], own_recv.at[t, p], (up, c))

    def down_copy(src, t, p):
        return send(src, t, own, t, p, down_send.at[t, p], own_recv.at[t, p], (down, c))

    def swap_copy(src, t, p):
        return send(src, t, other, t, p, swap_send.at[t, p], swap_recv.at[t, p], (beside, c))

    def put_rhs(src, t, p, offset):
        hi, lo = split(src[t, :, pl.ds(p * step, step)])
        at = pl.ds(pl.multiple_of(offset + p * step, 128), step)
        rhs_ref[pl.ds(t * depth, depth), at] = hi
        rhs_ref[pl.ds(pairs + t * depth, depth), at] = lo

    for p in range(PIECES):
        row_copy(1, p).start()
        row_copy(2, p).start()
    for t in range(groups):
        for p in range(PIECES):
            if t > 0:
                row_copy(t, p).wait_recv()
            if t == 2:
                row_copy(3, p).start()

            @pl.when(source)
            def _():
                swap_copy(rows, t, p).start()

                @pl.when(has_up)
                def _():
                    up_copy(rows, t, p).start()

                @pl.when(has_down)
                def _():
                    down_copy(rows, t, p).start()

                put_rhs(rows, t, p, place * width)

            @pl.when(jnp.logical_not(source))
            def _():
                up_copy(own, t, p).wait_recv()
                swap_copy(own, t, p).start()

                @pl.when(send_up)
                def _():
                    up_copy(own, t, p).start()

                @pl.when(send_down)
                def _():
                    down_copy(own, t, p).start()

                put_rhs(own, t, p, place * width)

            if t == groups - 1:
                w = jnp.concatenate(
                    [w_ref[pl.ds(pl.multiple_of(q * depth, depth), depth), :] for q in (c, core, chip, both)], axis=0
                )
                block = rows[:, :, pl.ds(p * step, step)].reshape(pairs, step)
                for f in range(w.shape[1]):
                    hi, lo = split((block * w[:, f:f + 1]).T)
                    at = pl.ds(p * step, step)
                    lhs_ref[f, at, 0:pairs] = hi
                    lhs_ref[f, at, pairs:2 * pairs] = hi
                    lhs_ref[f, at, 2 * pairs:] = lo
    for t in range(groups):
        for p in range(PIECES):
            swap_copy(own, t, p).wait_recv()
            put_rhs(other, t, p, (1 - place) * width)
    for t in range(groups):
        for p in range(PIECES):
            if t > 0:
                row_copy(t, p).wait_send()
            swap_copy(own, t, p).wait_send()

            @pl.when(send_up)
            def _():
                up_copy(own, t, p).wait_send()

            @pl.when(send_down)
            def _():
                down_copy(own, t, p).wait_send()


def gather(mel, weights, span):
    depth, width = mel.shape
    nf = weights.shape[1]
    dma = pltpu.SemaphoreType.DMA
    return pl.pallas_call(
        functools.partial(gather_kernel, span),
        out_shape=(
            jax.ShapeDtypeStruct((nf, width, 12 * depth), jnp.bfloat16),
            jax.ShapeDtypeStruct((8 * depth, span * width), jnp.bfloat16),
        ),
        in_specs=[pl.BlockSpec(memory_space=pltpu.VMEM), pl.BlockSpec(memory_space=pl.ANY)],
        out_specs=(pl.BlockSpec(memory_space=pltpu.VMEM), pl.BlockSpec(memory_space=pltpu.VMEM)),
        scratch_shapes=[pltpu.VMEM((4, depth, width), jnp.float32)] * 3
        + [dma, dma((3, PIECES)), dma((3, PIECES))]
        + [dma((4, PIECES))] * 5,
        compiler_params=pltpu.CompilerParams(
            collective_id=0, has_side_effects=True, vmem_limit_bytes=48 * 1024 * 1024
        ),
    )(weights, mel)


def product_kernel(lhs_ref, rhs_ref, out_ref):
    pairs = rhs_ref.shape[0] // 2
    rhs = rhs_ref[...]
    for f in range(out_ref.shape[0]):
        out_ref[f] = jnp.dot(
            lhs_ref[f], jnp.concatenate([rhs, rhs[:pairs]], axis=0), preferred_element_type=jnp.float32
        )


def product(lhs, rhs, tile=512):
    nf, height, depth = lhs.shape
    columns = rhs.shape[1]
    return pl.pallas_call(
        product_kernel,
        grid=(columns // tile,),
        out_shape=jax.ShapeDtypeStruct((nf, height, columns), jnp.float32),
        in_specs=[
            pl.BlockSpec((nf, height, depth), lambda i: (0, 0, 0), pipeline_mode=pl.Buffered(1)),
            pl.BlockSpec((rhs.shape[0], tile), lambda i: (0, i)),
        ],
        out_specs=pl.BlockSpec((nf, height, tile), lambda i: (0, 0, i)),
        compiler_params=pltpu.CompilerParams(vmem_limit_bytes=56 * 1024 * 1024),
    )(lhs, rhs)


def body(rows, cols, mel, pair_val, pair_cond, val_energy, cond_energy, freqs):
    weights = pair_weights(pair_val, pair_cond, val_energy, cond_energy, freqs)
    if cols == 4 and rows == 8 and mel.shape[0] % 16 == 0 and mel.shape[1] % (128 * PIECES) == 0:
        return product(*gather(mel, weights, rows // cols))
    rows_all = lax.all_gather(mel, "col", axis=0, tiled=True)
    own_block = lax.all_gather(mel, "row", axis=1, tiled=True)
    col_block = lax.all_to_all(own_block, "col", split_axis=1, concat_axis=0, tiled=True)
    scaled = weights.T[:, :, None] * rows_all[None, :, :]
    return lax.dot_general(
        scaled,
        col_block,
        (((1,), (0,)), ((), ())),
        precision=lax.Precision.HIGHEST,
        preferred_element_type=jnp.float32,
    )


def solution(mesh):
    return jax.shard_map(
        functools.partial(body, mesh.shape["row"], mesh.shape["col"]),
        mesh=mesh,
        in_specs=(P("col", "row"), P(), P(), P(), P(), P()),
        out_specs=P(None, "row", "col"),
        check_vma=False,
    )
```

time: 185 us -> 79.7 us (0.43)
  the two profiles are of different devices: /device:TPU:1 before, /device:TPU:5 now
where the time goes in v1:
time: 79.7 us; the launch traced here: 79.5 us
  Pallas kernels  75.5 us (95%)
  local copies, waits for them, and re-layouts  2.38 us (3%)
  other arithmetic  1.63 us (2%)
    pallas_call x1, Pallas kernels, gather(): pl.pallas_call(functools.partial(gather_kernel, span), out_shape=(jax.Sha...  41.6 us
    pallas_call x1, Pallas kernels, product(): pl.pallas_call(product_kernel, grid=(columns // tile,), out_shape=jax.Sha...  33.9 us
    unnamed x4, local copies, waits for them, and re-layouts  2.38 us

profile of v1, /device:TPU:5, one launch (start us, length us, event | category | flops | bytes accessed | tf_op | source)
XLA Modules:
  0.0 79.5 jit_solution(10486412434191386199)
XLA Ops:
  0.0 0.7 mul.52
  0.7 0.8 select_reduce_fusion
  1.5 0.1 divide_multiply_fusion.w_ref
  1.6 0.0 copy-start.1
  1.7 1.0 %copy-done.1 = f32[32,2304]{1,0:T(8,128)S(1)} copy-done((f32[32,2304]{1,0:T(8,128)S(1)}, f32[32,2304]{1,0:T(8,128)}, u32[]{:S(2)}) %copy-start.1) | copy-done | bytes 294936
  2.6 41.6 %shard_map.64 = (bf16[2,2304,384]{2,1,0:T(8,128)(2,1)}, bf16[256,4608]{1,0:T(8,128)(2,1)S(1)}) custom-call(f32[128,2]{1,0:T(8,128)S(1)} %divide_multiply_fusion.w_ref, f32[32,2304]{1,0:T(8,128)S(1)} %copy-done.1), custom_call_target="tpu_custom_call" | custom-call | tf_op jit(solution)/shard_map/pallas_call | solution.py:179
  44.2 0.0 copy-start
  44.2 1.4 %copy-done = bf16[256,4608]{1,0:T(8,128)(2,1)} copy-done((bf16[256,4608]{1,0:T(8,128)(2,1)}, bf16[256,4608]{1,0:T(8,128)(2,1)S(1)}, u32[]{:S(2)}) %copy-start) | copy-done | bytes 2359320
  45.6 33.9 %shard_map.65 = f32[2,2304,4608]{2,1,0:T(8,128)} custom-call(bf16[2,2304,384]{2,1,0:T(8,128)(2,1)} %get-tuple-element.7.lhs_ref, bf16[256,4608]{1,0:T(8,128)(2,1)} %copy-done), custom_call_target="tpu_custom_call" | custom-call | tf_op jit(solution)/shard_map/pallas_call | solution.py:208
  (1 shorter events, 0.0 us)
Async XLA Ops:
  1.6 1.0 %copy-start.1 = (f32[32,2304]{1,0:T(8,128)S(1)}, f32[32,2304]{1,0:T(8,128)}, u32[]{:S(2)}) copy-start(f32[32,2304]{1,0:T(8,128)} %mel_ref.1) | copy-start | bytes 884740
  44.2 1.4 %copy-start = (bf16[256,4608]{1,0:T(8,128)(2,1)}, bf16[256,4608]{1,0:T(8,128)(2,1)S(1)}, u32[]{:S(2)}) copy-start(bf16[256,4608]{1,0:T(8,128)(2,1)S(1)} %get-tuple-element.8.rhs_ref) | copy-start | bytes 7077892

commit v2 on v0

v2 whole, which is shorter than its diff:
```python
import functools
import math

import jax
import jax.numpy as jnp
from jax import lax
from jax.experimental import pallas as pl
from jax.experimental.pallas import tpu as pltpu
from jax.sharding import PartitionSpec as P

PAIRS = 128
MESH = pl.DeviceIdType.MESH
PIECES = 6
SWAPPED = 2
ALTERNATE = ((3,), (2, 3))
MIB = 1024 * 1024


def pair_weights(pair_val, pair_cond, val_energy, cond_energy, freqs):
    cond_onehot = (
        pair_cond[:, None] == jnp.arange(cond_energy.shape[0], dtype=jnp.int32)[None, :]
    ).astype(jnp.float32)
    val_onehot = (
        pair_val[:, None] == jnp.arange(val_energy.shape[0], dtype=jnp.int32)[None, :]
    ).astype(jnp.float32)
    gap = jnp.sum(cond_onehot * cond_energy[None, :], axis=1) - jnp.sum(
        val_onehot * val_energy[None, :], axis=1
    )
    scale = 1.0 / math.sqrt(PAIRS)
    return (
        -4.0
        * gap[None, :]
        / (gap[None, :] * gap[None, :] + freqs[:, None] * freqs[:, None])
        * scale
    )


def split(x):
    hi = x.astype(jnp.bfloat16)
    return hi, (x - hi.astype(jnp.float32)).astype(jnp.bfloat16)


def picked(energy, index):
    n = energy.shape[1]
    square = (n, n)
    eye = lax.broadcasted_iota(jnp.int32, square, 0) == lax.broadcasted_iota(jnp.int32, square, 1)
    column = jnp.sum(jnp.where(eye, energy, 0.0), axis=1, keepdims=True)
    onehot = lax.broadcasted_iota(jnp.int32, (n, index.shape[1]), 0) == index
    return jnp.sum(jnp.where(onehot, column, 0.0), axis=0, keepdims=True)


def gather_kernel(
    span, pv_ref, pc_ref, ve_ref, ce_ref, fr_ref, mel_ref, lhs_ref, rhs_ref, tail_ref, rows, own, other, alt,
    load_sem, row_send, row_recv, up_send, down_send, own_recv, swap_send, swap_recv,
    alt_up_send, alt_down_send, alt_recv, cross_send,
):
    r, c = lax.axis_index("row"), lax.axis_index("col")
    group, place = r // span, r % span
    depth, width = mel_ref.shape
    groups = 4
    pairs = groups * depth
    step = width // PIECES
    core = c + 1 - 2 * (c % 2)
    chip = c + 2 - 4 * (c // 2)
    both = core + 2 - 4 * (core // 2)
    order = (c, core, chip, both)
    alt_order = (chip, both, c, core)
    beside = r + 1 - 2 * place
    up, down = r + span, r - span
    has_up, has_down = group < groups - 1, group > 0
    source, alt_source = group == c, group == chip
    send_up, send_down = (group >= c) & has_up, (group <= c) & has_down
    alt_send_up, alt_send_down = (group >= chip) & has_up, (group <= chip) & has_down

    load = pltpu.make_async_copy(mel_ref, rows.at[c], load_sem)
    load.start()
    barrier = pltpu.get_barrier_semaphore()
    for device in ((r, core), (r, chip), (beside, c)):
        pl.semaphore_signal(barrier, inc=1, device_id=device, device_id_type=MESH)

    @pl.when(has_up)
    def _():
        pl.semaphore_signal(barrier, inc=1, device_id=(up, c), device_id_type=MESH)

    @pl.when(has_down)
    def _():
        pl.semaphore_signal(barrier, inc=1, device_id=(down, c), device_id_type=MESH)

    pl.semaphore_wait(barrier, 3 + has_up.astype(jnp.int32) + has_down.astype(jnp.int32))
    load.wait()

    def columns(p, offset=0):
        start = offset + p * step
        return pl.ds(start if isinstance(start, int) else pl.multiple_of(start, 128), step)

    def send(src, dst, q, p, send_sem, recv_sem, device):
        return pltpu.make_async_remote_copy(
            src_ref=src.at[q, :, columns(p)], dst_ref=dst.at[q, :, columns(p)], send_sem=send_sem, recv_sem=recv_sem,
            device_id=device, device_id_type=MESH,
        )

    def row_copy(t, p):
        device = (r, chip) if t == 2 else (r, core)
        return send(rows, rows, chip if t == 3 else c, p, row_send.at[t - 1, p], row_recv.at[t - 1, p], device)

    def up_copy(src, t, p):
        return send(src, own, order[t], p, up_send.at[t, p], own_recv.at[t, p], (up, c))

    def down_copy(src, t, p):
        return send(src, own, order[t], p, down_send.at[t, p], own_recv.at[t, p], (down, c))

    def swap_copy(src, t, p):
        return send(src, other, order[t], p, swap_send.at[t, p], swap_recv.at[t, p], (beside, c))

    def alt_up_copy(src, t, p):
        return send(src, alt, alt_order[t], p, alt_up_send.at[t - 2, p], alt_recv.at[t - 2, p], (up, c))

    def alt_down_copy(src, t, p):
        return send(src, alt, alt_order[t], p, alt_down_send.at[t - 2, p], alt_recv.at[t - 2, p], (down, c))

    def cross_copy(src, t, p):
        return send(src, own, alt_order[t], p, cross_send.at[t - 2, p], own_recv.at[t, p], (r, chip))

    def put_rhs(src, q, p, offset):
        hi, lo = split(src[q, :, columns(p)])
        at = columns(p, offset)
        first = pl.multiple_of(q * depth, depth)
        rhs_ref[pl.ds(first, depth), at] = hi
        rhs_ref[pl.ds(pl.multiple_of(pairs + q * depth, depth), depth), at] = lo

    def finish(src, t, p):
        if p < SWAPPED:
            swap_copy(src, t, p).start()
        else:
            first = pl.multiple_of(order[t] * depth, depth)
            tail_ref[pl.ds(first, depth), columns(p - SWAPPED)] = src[order[t], :, columns(p)]
        put_rhs(src, order[t], p, place * width)

    for p in range(PIECES):
        row_copy(2, p).start()
        row_copy(1, p).start()

    gap = picked(ce_ref[...], pc_ref[...]) - picked(ve_ref[...], pv_ref[...])
    scale = 1.0 / math.sqrt(PAIRS)
    weights = []
    for f in range(fr_ref.shape[1]):
        freq = fr_ref[:, f:f + 1]
        weights.append(-4.0 * gap / (gap * gap + freq * freq) * scale)

    for p in range(PIECES):
        away = ALTERNATE[p % len(ALTERNATE)]
        row_copy(1, p).wait_recv()
        for t in away:
            @pl.when(alt_source)
            def _():
                @pl.when(has_up)
                def _():
                    alt_up_copy(rows, t, p).start()

                @pl.when(has_down)
                def _():
                    alt_down_copy(rows, t, p).start()

        for t in range(groups):
            if t >= 2:
                row_copy(t, p).wait_recv()
            if t == 2:
                row_copy(3, p).start()

            @pl.when(source)
            def _():
                if t not in away:
                    @pl.when(has_up)
                    def _():
                        up_copy(rows, t, p).start()

                    @pl.when(has_down)
                    def _():
                        down_copy(rows, t, p).start()

                finish(rows, t, p)

            if t not in away:
                @pl.when(jnp.logical_not(source))
                def _():
                    up_copy(own, t, p).wait_recv()

                    @pl.when(send_up)
                    def _():
                        up_copy(own, t, p).start()

                    @pl.when(send_down)
                    def _():
                        down_copy(own, t, p).start()

                    finish(own, t, p)

        for t in away:
            @pl.when(jnp.logical_not(alt_source))
            def _():
                alt_up_copy(alt, t, p).wait_recv()

                @pl.when(alt_send_up)
                def _():
                    alt_up_copy(alt, t, p).start()

                @pl.when(alt_send_down)
                def _():
                    alt_down_copy(alt, t, p).start()

                cross_copy(alt, t, p).start()

        for t in ALTERNATE[(p - 1) % len(ALTERNATE)] if p > 0 else ():
            @pl.when(jnp.logical_not(source))
            def _():
                up_copy(own, t, p - 1).wait_recv()
                finish(own, t, p - 1)

        block = rows[:, :, columns(p)].reshape(pairs, step).T
        for f in range(fr_ref.shape[1]):
            hi, lo = split(block * weights[f])
            lhs_ref[f, columns(p), 0:pairs] = hi
            lhs_ref[f, columns(p), pairs:2 * pairs] = lo

    for t in ALTERNATE[(PIECES - 1) % len(ALTERNATE)]:
        @pl.when(jnp.logical_not(source))
        def _():
            up_copy(own, t, PIECES - 1).wait_recv()
            finish(own, t, PIECES - 1)

    for p in range(SWAPPED):
        for t in range(groups):
            swap_copy(own, t, p).wait_recv()
            put_rhs(other, order[t], p, (1 - place) * width)
    for p in range(PIECES):
        away = ALTERNATE[p % len(ALTERNATE)]
        for t in range(groups):
            if t > 0:
                row_copy(t, p).wait_send()
            if p < SWAPPED:
                swap_copy(own, t, p).wait_send()
            if t in away:
                @pl.when(alt_send_up)
                def _():
                    alt_up_copy(alt, t, p).wait_send()

                @pl.when(alt_send_down)
                def _():
                    alt_down_copy(alt, t, p).wait_send()

                @pl.when(jnp.logical_not(alt_source))
                def _():
                    cross_copy(alt, t, p).wait_send()
            else:
                @pl.when(send_up)
                def _():
                    up_copy(own, t, p).wait_send()

                @pl.when(send_down)
                def _():
                    down_copy(own, t, p).wait_send()


def gather(mel, small, span):
    depth, width = mel.shape
    nf = small[-1].shape[1]
    dma = pltpu.SemaphoreType.DMA
    four, two = dma((4, PIECES)), dma((2, PIECES))
    vmem = pl.BlockSpec(memory_space=pltpu.VMEM)
    return pl.pallas_call(
        functools.partial(gather_kernel, span),
        out_shape=(
            jax.ShapeDtypeStruct((nf, width, 8 * depth), jnp.bfloat16),
            jax.ShapeDtypeStruct((8 * depth, span * width), jnp.bfloat16),
            jax.ShapeDtypeStruct((4 * depth, width - SWAPPED * (width // PIECES)), jnp.float32),
        ),
        in_specs=[vmem] * 5 + [pl.BlockSpec(memory_space=pltpu.HBM)],
        out_specs=(vmem, vmem, vmem),
        scratch_shapes=[pltpu.VMEM((4, depth, width), jnp.float32)] * 4
        + [dma, dma((3, PIECES)), dma((3, PIECES))]
        + [four] * 5 + [two] * 4,
        compiler_params=pltpu.CompilerParams(
            collective_id=0, has_side_effects=True, vmem_limit_bytes=20 * MIB
        ),
    )(*small, mel)


def multiply(lhs_ref, rhs_hi, rhs_lo, out_ref):
    height = out_ref.shape[1]
    pairs = rhs_hi.shape[0]
    at = pl.ds(pl.multiple_of(pl.program_id(1) * height, height), height)
    right = jnp.concatenate([rhs_hi, rhs_hi, rhs_lo], axis=0)
    for f in range(out_ref.shape[0]):
        left = lhs_ref[f, at, :]
        out_ref[f] = jnp.dot(
            jnp.concatenate([left, left[:, :pairs]], axis=1), right, preferred_element_type=jnp.float32
        )


def first_kernel(place_ref, lhs_ref, rhs_ref, out_ref):
    pairs = rhs_ref.shape[0] // 2
    tile = out_ref.shape[2]
    count = rhs_ref.shape[1] // tile
    index = (pl.program_id(0) + place_ref[0] * (count // 2)) % count
    at = pl.ds(pl.multiple_of(index * tile, tile), tile)
    multiply(lhs_ref, rhs_ref[:pairs, at], rhs_ref[pairs:, at], out_ref)


def second_kernel(place_ref, lhs_ref, tail_ref, done_ref, out_ref):
    tile = out_ref.shape[2]
    at = pl.ds(pl.multiple_of(pl.program_id(0) * tile, tile), tile)
    hi, lo = split(tail_ref[:, at])
    multiply(lhs_ref, hi, lo, out_ref)


def product(lhs, rhs, tail, place, tail_of):
    nf, width, _ = lhs.shape
    columns = rhs.shape[1]
    tile = width // 3
    height = width // 2
    count = columns // tile
    last = tail.shape[1] // tile
    out = jax.ShapeDtypeStruct((nf, width, columns), jnp.float32)
    vmem = pl.BlockSpec(memory_space=pltpu.VMEM)

    def call(kernel, start, steps, operands, specs, aliases):
        flops = 2 * 3 * nf * width * PAIRS * tile * steps
        return pl.pallas_call(
            kernel,
            out_shape=out,
            grid_spec=pltpu.PrefetchScalarGridSpec(
                num_scalar_prefetch=1,
                grid=(steps, width // height),
                in_specs=specs,
                out_specs=pl.BlockSpec(
                    (nf, height, tile), lambda i, m, at: (0, m, (i + start + at[0] * (count // 2)) % count)
                ),
            ),
            input_output_aliases=aliases,
            cost_estimate=pl.CostEstimate(
                flops=flops, bytes_accessed=nf * width * tile * steps * 4, transcendentals=0
            ),
            compiler_params=pltpu.CompilerParams(vmem_limit_bytes=32 * MIB),
        )(place, *operands)

    done = call(first_kernel, 0, count - last, (lhs, rhs), [vmem, vmem], {})
    return call(
        second_kernel, count - last, last, (lhs, tail_of(tail), done), [vmem, vmem, pl.BlockSpec(memory_space=pl.ANY)], {3: 0}
    )


def body(rows, cols, mel, pair_val, pair_cond, val_energy, cond_energy, freqs):
    if cols == 4 and rows == 8 and mel.shape[0] % 16 == 0 and mel.shape[1] % (128 * PIECES) == 0:
        span = rows // cols
        small = [x[None, :] for x in (pair_val, pair_cond, val_energy, cond_energy, freqs)]
        place = (lax.axis_index("row") % span).astype(jnp.int32)[None]
        pairs = [(r, r + 1 - 2 * (r % span)) for r in range(rows)]
        return product(*gather(mel, small, span), place, lambda tail: lax.ppermute(tail, "row", pairs))
    weights = pair_weights(pair_val, pair_cond, val_energy, cond_energy, freqs)
    rows_all = lax.all_gather(mel, "col", axis=0, tiled=True)
    own_block = lax.all_gather(mel, "row", axis=1, tiled=True)
    col_block = lax.all_to_all(own_block, "col", split_axis=1, concat_axis=0, tiled=True)
    scaled = weights[:, :, None] * rows_all[None, :, :]
    return lax.dot_general(
        scaled,
        col_block,
        (((1,), (0,)), ((), ())),
        precision=lax.Precision.HIGHEST,
        preferred_element_type=jnp.float32,
    )


def solution(mesh):
    return jax.shard_map(
        functools.partial(body, mesh.shape["row"], mesh.shape["col"]),
        mesh=mesh,
        in_specs=(P("col", "row"), P(), P(), P(), P(), P()),
        out_specs=P(None, "row", "col"),
        check_vma=False,
    )
```

time: 185 us -> 107 us (0.58)
  Pallas kernels: 0 us -> 98.2 us
  waiting for transfers between devices: 87.2 us -> 0.01 us
  matrix products: 72.3 us -> 0 us
  between operations: 13.5 us -> 0.03 us
  starting transfers between devices: 5.98 us -> 0.67 us
  local copies, waits for them, and re-layouts: 4.89 us -> 7.3 us
    pallas_call x0 -> x3, Pallas kernels: none -> 98.2 us  [the longest x1 63.7 us: gather(): pl.pallas_call(functools.partial(gather_kernel, span), out_shape=(jax.Sha...]
    dot_general x1 -> x0, matrix products: 72.3 us -> none  [body(): lax.dot_general(scaled, col_block, (((1,), (0,)), ((), ())), precision=la...]
    all_gather x2 -> x0, waiting for transfers between devices: 70.1 us -> none  [the longest x1 53.9 us: body(): own_block = lax.all_gather(mel, 'row', axis=1, tiled=True)]
    all_to_all x1 -> x0, waiting for transfers between devices: 15.7 us -> none  [body(): lax.all_to_all(own_block, 'col', split_axis=1, concat_axis=0, tiled=True)]
    unnamed x10 -> x16, local copies, waits for them, and re-layouts: 0.02 us -> 7.3 us
    all_to_all x1 -> x0, starting transfers between devices: 5.94 us -> none  [body(): lax.all_to_all(own_block, 'col', split_axis=1, concat_axis=0, tiled=True)]
    all_to_all x1 -> x0, local copies, waits for them, and re-layouts: 3.24 us -> none  [body(): lax.all_to_all(own_block, 'col', split_axis=1, concat_axis=0, tiled=True)]
  transfers between devices with their start and end apart: 3 -> 1, of which waited for: 3 -> 0; matrix products, arithmetic and copies ran while one was open for 3% -> 0% of each run, Pallas kernels for 0% -> 21%
where the time goes in v2:
time: 107 us; the launch traced here: 106 us
  Pallas kernels  98.2 us (92%)
  local copies, waits for them, and re-layouts  7.3 us (7%)
    pallas_call x1, Pallas kernels, gather(): pl.pallas_call(functools.partial(gather_kernel, span), out_shape=(jax.Sha...  63.7 us
    pallas_call x2, Pallas kernels, call(): pl.pallas_call(kernel, out_shape=out, grid_spec=pltpu.PrefetchScalarGridS...  34.5 us
    unnamed x16, local copies, waits for them, and re-layouts  7.3 us
  transfers between devices with their start and end apart: 1, of which 0 were waited for; matrix products, arithmetic and copies ran while one was open for 0% of the time, Pallas kernels for 21%

profile of v2, /device:TPU:1, one launch (start us, length us, event | category | flops | bytes accessed | tf_op | source)
XLA Modules:
  0.0 106.2 jit_solution(7382153375149906874)
XLA Ops:
  0.0 0.0 copy-start.2
  0.0 1.0 copy-done.2
  1.0 0.0 copy-start.3
  1.0 0.7 copy-done.3
  1.6 0.0 copy-start.4
  1.6 0.7 copy-done.4
  2.3 0.0 copy-start.5
  2.3 0.7 copy-done.5
  2.9 0.0 copy-start.6
  2.9 0.7 copy-done.6
  3.6 0.0 copy-start.7
  3.6 0.7 copy-done.7
  4.2 63.7 %shard_map.64 = (bf16[2,2304,256]{2,1,0:T(8,128)(2,1)S(1)}, bf16[256,4608]{1,0:T(8,128)(2,1)S(1)}, f32[128,1536]{1,0:T(8,128)}) custom-call(s32[1,128]{1,0:T(1,128)S(1)} %bitcast.6, s32[1,128]{1,0:T(1,128)S(1)} %bitcast.7, f32[1,32]{1,0:T(1,128)S(1)} %bitcast.8, f32[1,32]{1,0:T(1,128)S(1)} %bitcast.9, f32[1,2]{1,0:T(1,128)S(1)} %bitcast.10, ...), custom_call_target="tpu_custom_call" | custom-call | tf_op jit(solution)/shard_map/pallas_call | solution.py:270
  68.0 0.0 copy-start
  68.0 1.4 %copy-done = bf16[256,4608]{1,0:T(8,128)(2,1)} copy-done((bf16[256,4608]{1,0:T(8,128)(2,1)}, bf16[256,4608]{1,0:T(8,128)(2,1)S(1)}, u32[]{:S(2)}) %copy-start) | copy-done | bytes 2359320
  69.4 0.7 collective-permute-start
  70.0 0.0 copy-start.1
  70.1 1.7 %copy-done.1 = bf16[256,4608]{1,0:T(8,128)(2,1)S(1)} copy-done((bf16[256,4608]{1,0:T(8,128)(2,1)S(1)}, bf16[256,4608]{1,0:T(8,128)(2,1)}, u32[]{:S(2)}) %copy-start.1) | copy-done | bytes 2359320
  71.7 22.2 %shard_map.65.done_ref = f32[2,2304,4608]{2,1,0:T(8,128)} custom-call(s32[1]{0:T(128)} %bitcast.place_ref, bf16[2,2304,256]{2,1,0:T(8,128)(2,1)S(1)} %get-tuple-element.8.lhs_ref, bf16[256,4608]{1,0:T(8,128)(2,1)S(1)} %copy-done.1), custom_call_target="tpu_custom_call" | custom-call | flops 10871635968 | bytes 56623104 | tf_op jit(solution)/shard_map/pallas_call | solution.py:328
  93.9 0.0 collective-permute-done.tail_ref
  93.9 12.3 %shard_map.66 = f32[2,2304,4608]{2,1,0:T(8,128)} custom-call(s32[1]{0:T(128)} %bitcast.place_ref, bf16[2,2304,256]{2,1,0:T(8,128)(2,1)S(1)} %get-tuple-element.8.lhs_ref, f32[128,1536]{1,0:T(8,128)S(1)} %collective-permute-done.tail_ref, f32[2,2304,4608]{2,1,0:T(8,128)} %shard_map.65.done_ref), custom_call_target="tpu_custom_call", output_to_operand_aliasing={{}: (3, {})} | custom-call | flops 5435817984 | bytes 28311552 | tf_op jit(solution)/shard_map/pallas_call | solution.py:328
Async XLA Ops:
  0.0 1.0 copy-start.2
  1.0 0.7 copy-start.3
  1.6 0.7 copy-start.4
  2.3 0.7 copy-start.5
  2.9 0.7 copy-start.6
  3.6 0.7 copy-start.7
  68.0 1.4 %copy-start = (bf16[256,4608]{1,0:T(8,128)(2,1)}, bf16[256,4608]{1,0:T(8,128)(2,1)S(1)}, u32[]{:S(2)}) copy-start(bf16[256,4608]{1,0:T(8,128)(2,1)S(1)} %get-tuple-element.10.rhs_ref) | copy-start | bytes 7077892
  69.4 24.5 %collective-permute-start = (f32[128,1536]{1,0:T(8,128)}, f32[128,1536]{1,0:T(8,128)S(1)}, u32[]{:S(2)}, u32[]{:S(2)}) collective-permute-start(f32[128,1536]{1,0:T(8,128)} %get-tuple-element.9), channel_id=1, source_target_pairs={{0,4},{4,0},{8,12},{12,8},{16,20},{20,16},{24,28},{28,24},{1,5},{5... | collective-permute-start | bytes 2359304 | tf_op jit(solution)/shard_map/ppermute | solution.py:358
  70.0 1.7 %copy-start.1 = (bf16[256,4608]{1,0:T(8,128)(2,1)S(1)}, bf16[256,4608]{1,0:T(8,128)(2,1)}, u32[]{:S(2)}) copy-start(bf16[256,4608]{1,0:T(8,128)(2,1)} %copy-done) | copy-start | bytes 7077892

commit v3 on v2

--- a/solution.py
+++ b/solution.py
@@ -12,6 +12,8 @@
 MESH = pl.DeviceIdType.MESH
 PIECES = 6
 SWAPPED = 2
+LEAD = 3
+CROSS_LAG = 2
 ALTERNATE = ((3,), (2, 3))
 MIB = 1024 * 1024
 
@@ -40,17 +42,8 @@
     return hi, (x - hi.astype(jnp.float32)).astype(jnp.bfloat16)
 
 
-def picked(energy, index):
-    n = energy.shape[1]
-    square = (n, n)
-    eye = lax.broadcasted_iota(jnp.int32, square, 0) == lax.broadcasted_iota(jnp.int32, square, 1)
-    column = jnp.sum(jnp.where(eye, energy, 0.0), axis=1, keepdims=True)
-    onehot = lax.broadcasted_iota(jnp.int32, (n, index.shape[1]), 0) == index
-    return jnp.sum(jnp.where(onehot, column, 0.0), axis=0, keepdims=True)
-
-
 def gather_kernel(
-    span, pv_ref, pc_ref, ve_ref, ce_ref, fr_ref, mel_ref, lhs_ref, rhs_ref, tail_ref, rows, own, other, alt,
+    span, w_ref, mel_ref, lhs_ref, rhs_ref, tail_ref, rows, own, other, alt,
     load_sem, row_send, row_recv, up_send, down_send, own_recv, swap_send, swap_recv,
     alt_up_send, alt_down_send, alt_recv, cross_send,
 ):
@@ -140,36 +133,19 @@
         row_copy(2, p).start()
         row_copy(1, p).start()
 
-    gap = picked(ce_ref[...], pc_ref[...]) - picked(ve_ref[...], pv_ref[...])
-    scale = 1.0 / math.sqrt(PAIRS)
-    weights = []
-    for f in range(fr_ref.shape[1]):
-        freq = fr_ref[:, f:f + 1]
-        weights.append(-4.0 * gap / (gap * gap + freq * freq) * scale)
-
-    for p in range(PIECES):
-        away = ALTERNATE[p % len(ALTERNATE)]
-        row_copy(1, p).wait_recv()
-        for t in away:
-            @pl.when(alt_source)
-            def _():
-                @pl.when(has_up)
-                def _():
-                    alt_up_copy(rows, t, p).start()
-
-                @pl.when(has_down)
-                def _():
-                    alt_down_copy(rows, t, p).start()
-
+    def away(p):
+        return ALTERNATE[p % len(ALTERNATE)]
+
+    def originate(p):
         for t in range(groups):
-            if t >= 2:
+            if t > 0:
                 row_copy(t, p).wait_recv()
             if t == 2:
                 row_copy(3, p).start()
 
             @pl.when(source)
             def _():
-                if t not in away:
+                if t not in away(p):
                     @pl.when(has_up)
                     def _():
                         up_copy(rows, t, p).start()
@@ -180,7 +156,20 @@
 
                 finish(rows, t, p)
 
-            if t not in away:
+            for s in away(p) if t == 1 else ():
+                @pl.when(alt_source)
+                def _():
+                    @pl.when(has_up)
+                    def _():
+                        alt_up_copy(rows, s, p).start()
+
+                    @pl.when(has_down)
+                    def _():
+                        alt_down_copy(rows, s, p).start()
+
+    def relay(p):
+        for t in range(groups):
+            if t not in away(p):
                 @pl.when(jnp.logical_not(source))
                 def _():
                     up_copy(own, t, p).wait_recv()
@@ -195,7 +184,7 @@
 
                     finish(own, t, p)
 
-        for t in away:
+        for t in away(p):
             @pl.when(jnp.logical_not(alt_source))
             def _():
                 alt_up_copy(alt, t, p).wait_recv()
@@ -210,36 +199,41 @@
 
                 cross_copy(alt, t, p).start()
 
-        for t in ALTERNATE[(p - 1) % len(ALTERNATE)] if p > 0 else ():
+    def crossed(p):
+        for t in away(p):
             @pl.when(jnp.logical_not(source))
             def _():
-                up_copy(own, t, p - 1).wait_recv()
-                finish(own, t, p - 1)
-
+                up_copy(own, t, p).wait_recv()
+                finish(own, t, p)
+
+    def put_lhs(p):
         block = rows[:, :, columns(p)].reshape(pairs, step).T
-        for f in range(fr_ref.shape[1]):
-            hi, lo = split(block * weights[f])
+        for f in range(w_ref.shape[0]):
+            hi, lo = split(block * w_ref[f:f + 1, :])
             lhs_ref[f, columns(p), 0:pairs] = hi
             lhs_ref[f, columns(p), pairs:2 * pairs] = lo
 
-    for t in ALTERNATE[(PIECES - 1) % len(ALTERNATE)]:
-        @pl.when(jnp.logical_not(source))
-        def _():
-            up_copy(own, t, PIECES - 1).wait_recv()
-            finish(own, t, PIECES - 1)
+    for turn in range(PIECES + LEAD + CROSS_LAG):
+        if turn < PIECES:
+            originate(turn)
+        if 0 <= turn - LEAD < PIECES:
+            relay(turn - LEAD)
+        if 0 <= turn - LEAD - CROSS_LAG < PIECES:
+            crossed(turn - LEAD - CROSS_LAG)
+        if 0 <= turn - LEAD < PIECES:
+            put_lhs(turn - LEAD)
 
     for p in range(SWAPPED):
         for t in range(groups):
             swap_copy(own, t, p).wait_recv()
             put_rhs(other, order[t], p, (1 - place) * width)
     for p in range(PIECES):
-        away = ALTERNATE[p % len(ALTERNATE)]
         for t in range(groups):
             if t > 0:
                 row_copy(t, p).wait_send()
             if p < SWAPPED:
                 swap_copy(own, t, p).wait_send()
-            if t in away:
+            if t in away(p):
                 @pl.when(alt_send_up)
                 def _():
                     alt_up_copy(alt, t, p).wait_send()
@@ -261,9 +255,9 @@
                     down_copy(own, t, p).wait_send()
 
 
-def gather(mel, small, span):
+def gather(mel, weights, span):
     depth, width = mel.shape
-    nf = small[-1].shape[1]
+    nf = weights.shape[0]
     dma = pltpu.SemaphoreType.DMA
     four, two = dma((4, PIECES)), dma((2, PIECES))
     vmem = pl.BlockSpec(memory_space=pltpu.VMEM)
@@ -274,7 +268,7 @@
             jax.ShapeDtypeStruct((8 * depth, span * width), jnp.bfloat16),
             jax.ShapeDtypeStruct((4 * depth, width - SWAPPED * (width // PIECES)), jnp.float32),
         ),
-        in_specs=[vmem] * 5 + [pl.BlockSpec(memory_space=pltpu.HBM)],
+        in_specs=[vmem, pl.BlockSpec(memory_space=pl.ANY)],
         out_specs=(vmem, vmem, vmem),
         scratch_shapes=[pltpu.VMEM((4, depth, width), jnp.float32)] * 4
         + [dma, dma((3, PIECES)), dma((3, PIECES))]
@@ -282,7 +276,7 @@
         compiler_params=pltpu.CompilerParams(
             collective_id=0, has_side_effects=True, vmem_limit_bytes=20 * MIB
         ),
-    )(*small, mel)
+    )(weights, mel)
 
 
 def multiply(lhs_ref, rhs_hi, rhs_lo, out_ref):
@@ -306,7 +300,7 @@
     multiply(lhs_ref, rhs_ref[:pairs, at], rhs_ref[pairs:, at], out_ref)
 
 
-def second_kernel(place_ref, lhs_ref, tail_ref, done_ref, out_ref):
+def second_kernel(place_ref, lhs_ref, tail_ref, rhs_ref, done_ref, out_ref):
     tile = out_ref.shape[2]
     at = pl.ds(pl.multiple_of(pl.program_id(0) * tile, tile), tile)
     hi, lo = split(tail_ref[:, at])
@@ -345,18 +339,18 @@
 
     done = call(first_kernel, 0, count - last, (lhs, rhs), [vmem, vmem], {})
     return call(
-        second_kernel, count - last, last, (lhs, tail_of(tail), done), [vmem, vmem, pl.BlockSpec(memory_space=pl.ANY)], {3: 0}
+        second_kernel, count - last, last, (lhs, tail_of(tail), rhs, done),
+        [vmem] * 3 + [pl.BlockSpec(memory_space=pl.ANY)], {4: 0},
     )
 
 
 def body(rows, cols, mel, pair_val, pair_cond, val_energy, cond_energy, freqs):
+    weights = pair_weights(pair_val, pair_cond, val_energy, cond_energy, freqs)
     if cols == 4 and rows == 8 and mel.shape[0] % 16 == 0 and mel.shape[1] % (128 * PIECES) == 0:
         span = rows // cols
-        small = [x[None, :] for x in (pair_val, pair_cond, val_energy, cond_energy, freqs)]
         place = (lax.axis_index("row") % span).astype(jnp.int32)[None]
         pairs = [(r, r + 1 - 2 * (r % span)) for r in range(rows)]
-        return product(*gather(mel, small, span), place, lambda tail: lax.ppermute(tail, "row", pairs))
-    weights = pair_weights(pair_val, pair_cond, val_energy, cond_energy, freqs)
+        return product(*gather(mel, weights, span), place, lambda tail: lax.ppermute(tail, "row", pairs))
     rows_all = lax.all_gather(mel, "col", axis=0, tiled=True)
     own_block = lax.all_gather(mel, "row", axis=1, tiled=True)
     col_block = lax.all_to_all(own_block, "col", split_axis=1, concat_axis=0, tiled=True)

time: 107 us -> 80.6 us (0.75)
  Pallas kernels: 98.2 us -> 73.5 us
  local copies, waits for them, and re-layouts: 7.3 us -> 4.03 us
  other arithmetic: 0 us -> 1.61 us
    pallas_call x1, Pallas kernels: 63.7 us -> 39 us  [gather(): pl.pallas_call(functools.partial(gather_kernel, span), out_shape=(jax.Sha...]
    unnamed x16 -> x6, local copies, waits for them, and re-layouts: 7.3 us -> 4.03 us
  transfers between devices with their start and end apart: 1 -> 1, of which waited for: 0 -> 0; matrix products, arithmetic and copies ran while one was open for 0% -> 0% of each run, Pallas kernels for 21% -> 28%
where the time goes in v3:
time: 80.6 us; the launch traced here: 80.4 us
  Pallas kernels  73.5 us (91%)
  local copies, waits for them, and re-layouts  4.03 us (5%)
  other arithmetic  1.61 us (2%)
  starting transfers between devices  1.21 us (2%)
    pallas_call x1, Pallas kernels, gather(): pl.pallas_call(functools.partial(gather_kernel, span), out_shape=(jax.Sha...  39 us
    pallas_call x2, Pallas kernels, call(): pl.pallas_call(kernel, out_shape=out, grid_spec=pltpu.PrefetchScalarGridS...  34.5 us
    unnamed x6, local copies, waits for them, and re-layouts  4.03 us
  transfers between devices with their start and end apart: 1, of which 0 were waited for; matrix products, arithmetic and copies ran while one was open for 0% of the time, Pallas kernels for 28%

profile of v3, /device:TPU:1, one launch (start us, length us, event | category | flops | bytes accessed | tf_op | source)
XLA Modules:
  0.0 80.4 jit_solution(11106446188357693803)
XLA Ops:
  0.0 0.7 mul.52
  0.7 0.8 select_reduce_fusion
  1.5 0.1 divide_multiply_fusion.w_ref
  1.6 0.0 copy-start.2
  1.6 1.0 %copy-done.2 = f32[32,2304]{1,0:T(8,128)S(1)} copy-done((f32[32,2304]{1,0:T(8,128)S(1)}, f32[32,2304]{1,0:T(8,128)}, u32[]{:S(2)}) %copy-start.2) | copy-done | bytes 294936
  2.6 39.0 %shard_map.64 = (bf16[2,2304,256]{2,1,0:T(8,128)(2,1)S(1)}, bf16[256,4608]{1,0:T(8,128)(2,1)S(1)}, f32[128,1536]{1,0:T(8,128)}) custom-call(f32[2,128]{1,0:T(2,128)S(1)} %divide_multiply_fusion.w_ref, f32[32,2304]{1,0:T(8,128)S(1)} %copy-done.2), custom_call_target="tpu_custom_call" | custom-call | tf_op jit(solution)/shard_map/pallas_call | solution.py:264
  41.6 0.0 copy-start
  41.6 1.4 %copy-done = bf16[256,4608]{1,0:T(8,128)(2,1)} copy-done((bf16[256,4608]{1,0:T(8,128)(2,1)}, bf16[256,4608]{1,0:T(8,128)(2,1)S(1)}, u32[]{:S(2)}) %copy-start) | copy-done | bytes 2359320
  43.0 1.2 %collective-permute-start = (f32[128,1536]{1,0:T(8,128)}, f32[128,1536]{1,0:T(8,128)S(1)}, u32[]{:S(2)}, u32[]{:S(2)}) collective-permute-start(f32[128,1536]{1,0:T(8,128)} %get-tuple-element.9), channel_id=1, source_target_pairs={{0,4},{4,0},{8,12},{12,8},{16,20},{20,16},{24,28},{28,24},{1,5},{5... | collective-permute-start | bytes 2359304 | tf_op jit(solution)/shard_map/ppermute | solution.py:353
  44.2 0.0 copy-start.1
  44.2 1.7 %copy-done.1 = bf16[256,4608]{1,0:T(8,128)(2,1)S(1)} copy-done((bf16[256,4608]{1,0:T(8,128)(2,1)S(1)}, bf16[256,4608]{1,0:T(8,128)(2,1)}, u32[]{:S(2)}) %copy-start.1) | copy-done | bytes 2359320
  45.9 22.2 %shard_map.65.done_ref = f32[2,2304,4608]{2,1,0:T(8,128)} custom-call(s32[1]{0:T(128)} %bitcast.place_ref, bf16[2,2304,256]{2,1,0:T(8,128)(2,1)S(1)} %get-tuple-element.8.lhs_ref, bf16[256,4608]{1,0:T(8,128)(2,1)S(1)} %copy-done.1), custom_call_target="tpu_custom_call" | custom-call | flops 10871635968 | bytes 56623104 | tf_op jit(solution)/shard_map/pallas_call | solution.py:322
  68.1 0.0 collective-permute-done.tail_ref
  68.1 12.3 %shard_map.66 = f32[2,2304,4608]{2,1,0:T(8,128)} custom-call(s32[1]{0:T(128)} %bitcast.place_ref, bf16[2,2304,256]{2,1,0:T(8,128)(2,1)S(1)} %get-tuple-element.8.lhs_ref, f32[128,1536]{1,0:T(8,128)S(1)} %collective-permute-done.tail_ref, bf16[256,4608]{1,0:T(8,128)(2,1)S(1)} %copy-done.1, ...), custom_call_target="tpu_custom_call", output_to_operand_aliasing={{}: (4, {})} | custom-call | flops 5435817984 | bytes 28311552 | tf_op jit(solution)/shard_map/pallas_call | solution.py:322
  (1 shorter events, 0.0 us)
Async XLA Ops:
  1.6 1.0 %copy-start.2 = (f32[32,2304]{1,0:T(8,128)S(1)}, f32[32,2304]{1,0:T(8,128)}, u32[]{:S(2)}) copy-start(f32[32,2304]{1,0:T(8,128)} %mel_ref.1) | copy-start | bytes 884740
  41.6 1.4 %copy-start = (bf16[256,4608]{1,0:T(8,128)(2,1)}, bf16[256,4608]{1,0:T(8,128)(2,1)S(1)}, u32[]{:S(2)}) copy-start(bf16[256,4608]{1,0:T(8,128)(2,1)S(1)} %get-tuple-element.10.rhs_ref) | copy-start | bytes 7077892
  43.0 25.1 %collective-permute-start = (f32[128,1536]{1,0:T(8,128)}, f32[128,1536]{1,0:T(8,128)S(1)}, u32[]{:S(2)}, u32[]{:S(2)}) collective-permute-start(f32[128,1536]{1,0:T(8,128)} %get-tuple-element.9), channel_id=1, source_target_pairs={{0,4},{4,0},{8,12},{12,8},{16,20},{20,16},{24,28},{28,24},{1,5},{5... | collective-permute-start | bytes 2359304 | tf_op jit(solution)/shard_map/ppermute | solution.py:353
  44.2 1.7 %copy-start.1 = (bf16[256,4608]{1,0:T(8,128)(2,1)S(1)}, bf16[256,4608]{1,0:T(8,128)(2,1)}, u32[]{:S(2)}) copy-start(bf16[256,4608]{1,0:T(8,128)(2,1)} %copy-done) | copy-start | bytes 7077892

commit v4 on v3

--- a/solution.py
+++ b/solution.py
@@ -10,10 +10,10 @@
 
 PAIRS = 128
 MESH = pl.DeviceIdType.MESH
-PIECES = 6
-SWAPPED = 2
+PIECES = 3
+SWAPPED = 1
 LEAD = 3
-CROSS_LAG = 2
+CROSS_LAG = 1
 ALTERNATE = ((3,), (2, 3))
 MIB = 1024 * 1024
 

time: 80.6 us -> 77.8 us (0.965)
  Pallas kernels: 73.5 us -> 70.7 us
    pallas_call x1, Pallas kernels: 39 us -> 36.2 us  [gather(): pl.pallas_call(functools.partial(gather_kernel, span), out_shape=(jax.Sha...]
  transfers between devices with their start and end apart: 1 -> 1, of which waited for: 0 -> 0; matrix products, arithmetic and copies ran while one was open for 0% -> 0% of each run, Pallas kernels for 28% -> 29%
where the time goes in v4:
time: 77.8 us; the launch traced here: 77.6 us
  Pallas kernels  70.7 us (91%)
  local copies, waits for them, and re-layouts  4.03 us (5%)
  other arithmetic  1.61 us (2%)
  starting transfers between devices  1.21 us (2%)
    pallas_call x1, Pallas kernels, gather(): pl.pallas_call(functools.partial(gather_kernel, span), out_shape=(jax.Sha...  36.2 us
    pallas_call x2, Pallas kernels, call(): pl.pallas_call(kernel, out_shape=out, grid_spec=pltpu.PrefetchScalarGridS...  34.5 us
    unnamed x6, local copies, waits for them, and re-layouts  4.03 us
  transfers between devices with their start and end apart: 1, of which 0 were waited for; matrix products, arithmetic and copies ran while one was open for 0% of the time, Pallas kernels for 29%

profile of v4, /device:TPU:1, one launch (start us, length us, event | category | flops | bytes accessed | tf_op | source)
XLA Modules:
  0.0 77.6 jit_solution(8107146029770480838)
XLA Ops:
  0.0 0.7 mul.52
  0.7 0.8 %select_reduce_fusion = (f32[128]{0:T(128)S(1)}, f32[128]{0:T(128)S(1)}) fusion(f32[32]{0:T(128)} %param.9, s32[128]{0:T(128)} %param.7, f32[32]{0:T(128)} %param.10, s32[128]{0:T(128)} %param.8), kind=kLoop, calls=%fused_computation | loop fusion | flops 24320 | bytes 2304 | tf_op jit(solution)/shard_map/reduce_sum | solution.py:28
  1.5 0.1 divide_multiply_fusion.w_ref
  1.6 0.0 copy-start.2
  1.6 1.0 %copy-done.2 = f32[32,2304]{1,0:T(8,128)S(1)} copy-done((f32[32,2304]{1,0:T(8,128)S(1)}, f32[32,2304]{1,0:T(8,128)}, u32[]{:S(2)}) %copy-start.2) | copy-done | bytes 294936
  2.6 36.2 %shard_map.64 = (bf16[2,2304,256]{2,1,0:T(8,128)(2,1)S(1)}, bf16[256,4608]{1,0:T(8,128)(2,1)S(1)}, f32[128,1536]{1,0:T(8,128)}) custom-call(f32[2,128]{1,0:T(2,128)S(1)} %divide_multiply_fusion.w_ref, f32[32,2304]{1,0:T(8,128)S(1)} %copy-done.2), custom_call_target="tpu_custom_call" | custom-call | tf_op jit(solution)/shard_map/pallas_call | solution.py:264
  38.8 0.0 copy-start
  38.8 1.4 %copy-done = bf16[256,4608]{1,0:T(8,128)(2,1)} copy-done((bf16[256,4608]{1,0:T(8,128)(2,1)}, bf16[256,4608]{1,0:T(8,128)(2,1)S(1)}, u32[]{:S(2)}) %copy-start) | copy-done | bytes 2359320
  40.2 1.2 %collective-permute-start = (f32[128,1536]{1,0:T(8,128)}, f32[128,1536]{1,0:T(8,128)S(1)}, u32[]{:S(2)}, u32[]{:S(2)}) collective-permute-start(f32[128,1536]{1,0:T(8,128)} %get-tuple-element.9), channel_id=1, source_target_pairs={{0,4},{4,0},{8,12},{12,8},{16,20},{20,16},{24,28},{28,24},{1,5},{5... | collective-permute-start | bytes 2359304 | tf_op jit(solution)/shard_map/ppermute | solution.py:353
  41.4 0.0 copy-start.1
  41.4 1.7 %copy-done.1 = bf16[256,4608]{1,0:T(8,128)(2,1)S(1)} copy-done((bf16[256,4608]{1,0:T(8,128)(2,1)S(1)}, bf16[256,4608]{1,0:T(8,128)(2,1)}, u32[]{:S(2)}) %copy-start.1) | copy-done | bytes 2359320
  43.1 22.2 %shard_map.65.done_ref = f32[2,2304,4608]{2,1,0:T(8,128)} custom-call(s32[1]{0:T(128)} %bitcast.place_ref, bf16[2,2304,256]{2,1,0:T(8,128)(2,1)S(1)} %get-tuple-element.8.lhs_ref, bf16[256,4608]{1,0:T(8,128)(2,1)S(1)} %copy-done.1), custom_call_target="tpu_custom_call" | custom-call | flops 10871635968 | bytes 56623104 | tf_op jit(solution)/shard_map/pallas_call | solution.py:322
  65.3 0.0 collective-permute-done.tail_ref
  65.3 12.3 %shard_map.66 = f32[2,2304,4608]{2,1,0:T(8,128)} custom-call(s32[1]{0:T(128)} %bitcast.place_ref, bf16[2,2304,256]{2,1,0:T(8,128)(2,1)S(1)} %get-tuple-element.8.lhs_ref, f32[128,1536]{1,0:T(8,128)S(1)} %collective-permute-done.tail_ref, bf16[256,4608]{1,0:T(8,128)(2,1)S(1)} %copy-done.1, ...), custom_call_target="tpu_custom_call", output_to_operand_aliasing={{}: (4, {})} | custom-call | flops 5435817984 | bytes 28311552 | tf_op jit(solution)/shard_map/pallas_call | solution.py:322
  (1 shorter events, 0.0 us)
Async XLA Ops:
  1.6 1.0 %copy-start.2 = (f32[32,2304]{1,0:T(8,128)S(1)}, f32[32,2304]{1,0:T(8,128)}, u32[]{:S(2)}) copy-start(f32[32,2304]{1,0:T(8,128)} %mel_ref.1) | copy-start | bytes 884740
  38.8 1.4 %copy-start = (bf16[256,4608]{1,0:T(8,128)(2,1)}, bf16[256,4608]{1,0:T(8,128)(2,1)S(1)}, u32[]{:S(2)}) copy-start(bf16[256,4608]{1,0:T(8,128)(2,1)S(1)} %get-tuple-element.10.rhs_ref) | copy-start | bytes 7077892
  40.2 25.1 %collective-permute-start = (f32[128,1536]{1,0:T(8,128)}, f32[128,1536]{1,0:T(8,128)S(1)}, u32[]{:S(2)}, u32[]{:S(2)}) collective-permute-start(f32[128,1536]{1,0:T(8,128)} %get-tuple-element.9), channel_id=1, source_target_pairs={{0,4},{4,0},{8,12},{12,8},{16,20},{20,16},{24,28},{28,24},{1,5},{5... | collective-permute-start | bytes 2359304 | tf_op jit(solution)/shard_map/ppermute | solution.py:353
  41.4 1.7 %copy-start.1 = (bf16[256,4608]{1,0:T(8,128)(2,1)S(1)}, bf16[256,4608]{1,0:T(8,128)(2,1)}, u32[]{:S(2)}) copy-start(bf16[256,4608]{1,0:T(8,128)(2,1)} %copy-done) | copy-start | bytes 7077892
